TPU v7x, 128 devices: a whole 4x4x4 slice. The times are simulated.
128 devices in a mesh: var: 16 (over x_hi, z, core), tp: 8 (over y, x_lo).
Axes of the slice: x: 4 (x_hi: 2, x_lo: 2; x = x_hi * 2 + x_lo), y: 4, z: 4, core: 2. Of those that a mesh axis runs over, the one named last changes fastest.
Arguments:
- hidden_in: bfloat16 [48, 384, 2048], P('var'), may hold values from -100 to 100
- run_table: int32 [48, 2], P('var'), may hold values 0 or 1
- qkv_weight: bfloat16 [2048, 3072], P('var', 'tp'), may hold values from -1 to 1
- out_weight: bfloat16 [2048, 2048], P('tp', 'var'), may hold values from -0.125 to 0.125
- gate_up_weight: bfloat16 [2048, 2, 8192], P('var', None, 'tp'), may hold values from -0.125 to 0.125
- down_weight: bfloat16 [8192, 2048], P('tp', 'var'), may hold values from -0.0625 to 0.0625
Outputs:
- layer_out: bfloat16 [48, 384, 2048], P('var')
All inputs are finite; a program needn't handle non-finite values. No bound on the sum of `run_table` on one device may be relied on, other than what follows from the above.
Results may differ from a plain program's by a relative error of at most 0.0075.
Values may be sent and summed in bfloat16 or wider, within the bound.
No kernel may reach another device: no remote copies, remote signals or barrier semaphores. Data moves between devices by JAX's collectives and lax.ppermute only.
A program may use at most 128 MiB of HBM per device.

v0:
```python
import jax
import jax.numpy as jnp
from jax import lax
from jax.sharding import PartitionSpec as P

QUERY_HEADS = 32
KEY_VALUE_HEADS = 8
HEAD_SIZE = 64


def rms_norm(tensor):
    widened = tensor.astype(jnp.float32)
    scaled = widened * lax.rsqrt(jnp.mean(widened * widened, axis=-1, keepdims=True) + 1e-05)
    return scaled.astype(jnp.bfloat16)


def rotary_embedding(tensor, token_positions):
    half_width = tensor.shape[-1] // 2
    exponent = jnp.arange(half_width, dtype=jnp.float32) * (2.0 / tensor.shape[-1])
    frequency = jnp.power(jnp.float32(500000.0), -exponent)
    angles = token_positions[:, None, None] * frequency[None, None, :]
    cosine = jnp.cos(angles)
    sine_part = jnp.sin(angles)
    first_half = tensor[..., :half_width]
    second_half = tensor[..., half_width:]
    return jnp.concatenate(
        [
            first_half * cosine - second_half * sine_part,
            second_half * cosine + first_half * sine_part,
        ],
        axis=-1,
    )


def attend(query_rows, keys_bfloat, values_bfloat, score_scale):
    scores = (
        jnp.einsum("bqkgd,bpkd->bkgqp", query_rows, keys_bfloat, preferred_element_type=jnp.float32)
        * score_scale
    )
    length = scores.shape[-1]
    causal = jnp.arange(length)[:, None] >= jnp.arange(length)[None, :]
    scores = jnp.where(causal, scores, jnp.float32(-1e30))
    row_max = jnp.max(scores, axis=-1, keepdims=True)
    exped = jnp.exp(scores - row_max)
    weights_bf = (exped / jnp.sum(exped, axis=-1, keepdims=True)).astype(jnp.bfloat16)
    head_outputs = jnp.einsum(
        "bkgqp,bpkd->bqkgd", weights_bf, values_bfloat, preferred_element_type=jnp.float32
    )
    return head_outputs.astype(jnp.bfloat16)


def shards(hidden_in, run_table, qkv_weight, out_weight, gate_up_weight, down_weight):
    tensor_parallel_count = lax.axis_size("tp")
    seq_count, full_len, model_width = hidden_in.shape
    row_count = seq_count * full_len
    query_slice = QUERY_HEADS // tensor_parallel_count
    key_value_slice = KEY_VALUE_HEADS // tensor_parallel_count
    group_width = QUERY_HEADS // KEY_VALUE_HEADS
    switches = run_table.astype(jnp.float32)
    flat_input = rms_norm(hidden_in).reshape(row_count, model_width)
    columns = flat_input
    projected_rows = jnp.dot(
        columns,
        lax.all_gather(qkv_weight, "var", axis=0, tiled=True),
        preferred_element_type=jnp.float32,
    )
    projected_rows = projected_rows.reshape(
        seq_count, full_len, query_slice + 2 * key_value_slice, HEAD_SIZE
    )
    token_positions = jnp.arange(full_len, dtype=jnp.float32)
    query_rows = rotary_embedding(projected_rows[:, :, :query_slice], token_positions).astype(
        jnp.bfloat16
    )
    query_rows = query_rows.reshape(seq_count, full_len, key_value_slice, group_width, HEAD_SIZE)
    keys_bfloat = rotary_embedding(
        projected_rows[:, :, query_slice : query_slice + key_value_slice], token_positions
    ).astype(jnp.bfloat16)
    values_bfloat = projected_rows[:, :, query_slice + key_value_slice :].astype(jnp.bfloat16)
    score_scale = HEAD_SIZE ** (-0.5)
    head_outputs = attend(query_rows, keys_bfloat, values_bfloat, score_scale)
    head_rows = head_outputs.reshape(row_count, query_slice * HEAD_SIZE)
    attn_terms = jnp.dot(
        head_rows,
        lax.all_gather(out_weight, "var", axis=1, tiled=True),
        preferred_element_type=jnp.float32,
    )
    attn_terms = attn_terms.reshape(seq_count, full_len, model_width)
    attn_switch = switches[:, 0][:, None, None]
    attention = lax.psum(attn_terms.astype(jnp.bfloat16), "tp").astype(jnp.float32)
    whole_after = (hidden_in.astype(jnp.float32) + attn_switch * attention).astype(jnp.bfloat16)
    mlp_input = rms_norm(whole_after)
    flat_mlp = mlp_input.reshape(row_count, model_width)
    ff_local = gate_up_weight.shape[2]
    block_piece = lax.all_gather(gate_up_weight, "var", axis=0, tiled=True)
    columns = flat_mlp
    flat_piece = block_piece.reshape(block_piece.shape[0], 2 * ff_local)
    gate_and_up = jnp.dot(columns, flat_piece, preferred_element_type=jnp.float32)
    hidden = (jax.nn.silu(gate_and_up[:, :ff_local]) * gate_and_up[:, ff_local:]).astype(
        jnp.bfloat16
    )
    mlp_terms = jnp.dot(
        hidden,
        lax.all_gather(down_weight, "var", axis=1, tiled=True),
        preferred_element_type=jnp.float32,
    )
    mlp_terms = mlp_terms.reshape(seq_count, full_len, model_width)
    mlp = lax.psum(mlp_terms.astype(jnp.bfloat16), "tp").astype(jnp.float32)
    mlp_switch = switches[:, 1][:, None, None]
    return (whole_after.astype(jnp.float32) + mlp_switch * mlp).astype(jnp.bfloat16)


def solution(mesh):
    return jax.shard_map(
        shards,
        mesh=mesh,
        in_specs=(
            P("var", None, None),
            P("var", None),
            P("var", "tp"),
            P("tp", "var"),
            P("var", None, "tp"),
            P("tp", "var"),
        ),
        out_specs=P("var", None, None),
        check_vma=False,
    )
```

profile of v0, /device:TPU:1, one launch (start us, length us, event | category | flops | bytes accessed | tf_op | source)
XLA Modules:
  0.0 667.6 jit_solution(8248139366592149826)
XLA Ops:
  6.5 0.7 all-gather.5.cloned.1.call-update
  7.3 0.7 all-gather.7.cloned.1.call-update
  8.1 3.3 fusion
  11.7 47.8 %all-gather.5.cloned.1.call-done = bf16[2048,384]{1,0:T(8,128)(2,1)} async-done(((bf16[128,384]{1,0:T(8,128)(2,1)}), bf16[2048,384]{1,0:T(8,128)(2,1)}) %all-gather.5.cloned.1.call-update) | async-done | bytes 1572880 | tf_op jit(solution)/shard_map/all_gather | solution.py:64
  59.5 1.7 copy.14
  61.2 4.6 fusion.9
  66.1 1.2 fusion.7
  67.3 1.5 fusion.6
  68.8 2.1 fusion.17
  70.9 32.4 %all-gather.7.cloned.1.call-done = bf16[256,2048]{1,0:T(8,128)(2,1)} async-done(((bf16[256,128]{1,0:T(8,128)(2,1)}), bf16[256,2048]{1,0:T(8,128)(2,1)}) %all-gather.7.cloned.1.call-update) | async-done | bytes 1048592 | tf_op jit(solution)/shard_map/all_gather | solution.py:84
  103.3 4.8 convolution_convert_fusion.1
  108.2 0.5 all-gather.9.cloned.1.call-update
  108.8 0.5 all-gather.11.cloned.1.call-update
  109.6 200.1 %all-reduce.3.cloned.1.call-done = bf16[3,384,2048]{2,1,0:T(8,128)(2,1)} async-done(((bf16[3,384,2048]{2,1,0:T(8,128)(2,1)}), bf16[3,384,2048]{2,1,0:T(8,128)(2,1)}) %all-reduce.3.cloned.1.call-update) | async-done | bytes 4718608 | tf_op jit(solution)/shard_map/psum | solution.py:89
  309.6 6.5 fusion.3
  316.1 2.2 copy-done
  318.3 3.0 fusion.4
  321.3 64.5 %all-gather.9.cloned.1.call-done = bf16[2048,2,1024]{2,1,0:T(2,128)(2,1)} async-done(((bf16[128,2,1024]{2,1,0:T(2,128)(2,1)}), bf16[2048,2,1024]{2,1,0:T(2,128)(2,1)}) %all-gather.9.cloned.1.call-update) | async-done | bytes 8388624 | tf_op jit(solution)/shard_map/all_gather | solution.py:94
  385.8 10.4 %copy.27 = bf16[256,8,2,1024]{3,1,2,0:T(8,128)(2,1)} copy(bf16[256,8,2,1024]{3,2,1,0:T(2,128)(2,1)} %bitcast.97) | data formatting | bytes 16777216
  396.1 14.6 %fusion.41 = f32[1152,2048]{1,0:T(8,128)} fusion(bf16[1152,2048]{1,0:T(8,128)(2,1)S(1)} %bitcast.100, bf16[2048,2048]{1,0:T(8,128)(2,1)} %bitcast.98), kind=kOutput, calls=%fused_computation.62 | convolution fusion | flops 9663676416 | bytes 22544384 | tf_op jit(solution)/shard_map/dot_general | solution.py:97
  410.8 31.4 %all-gather.11.cloned.1.call-done = bf16[1024,2048]{1,0:T(8,128)(2,1)} async-done(((bf16[1024,128]{1,0:T(8,128)(2,1)}), bf16[1024,2048]{1,0:T(8,128)(2,1)}) %all-gather.11.cloned.1.call-update) | async-done | bytes 4194320 | tf_op jit(solution)/shard_map/all_gather | solution.py:103
  442.2 10.4 %convolution_convert_fusion = bf16[1152,2048]{1,0:T(8,128)(2,1)} fusion(bf16[1024,2048]{1,0:T(8,128)(2,1)} %all-gather.11.cloned.1.call-done, f32[1152,2048]{1,0:T(8,128)} %fusion.41), kind=kOutput, calls=%fused_computation.12 | convolution fusion | flops 4841275392 | bytes 18350080 | tf_op jit(solution)/shard_map/dot_general | solution.py:101
  452.6 199.2 %all-reduce.5.cloned.1.call-done = bf16[3,384,2048]{2,1,0:T(8,128)(2,1)} async-done(((bf16[3,384,2048]{2,1,0:T(8,128)(2,1)}), bf16[3,384,2048]{2,1,0:T(8,128)(2,1)}) %all-reduce.5.cloned.1.call-update) | async-done | bytes 4718608 | tf_op jit(solution)/shard_map/psum | solution.py:107
  651.8 8.9 %fusion.5 = bf16[3,384,2048]{2,1,0:T(8,128)(2,1)} fusion(bf16[3,384,2048]{2,1,0:T(8,128)(2,1)} %copy-done, bf16[3,384,2048]{2,1,0:T(8,128)(2,1)} %all-reduce.5.cloned.1.call-done, f32[3]{0:T(128)S(1)} %get-tuple-element.9), kind=kLoop, calls=%fused_computation.11 | loop fusion | flops 11796480 | bytes 14155788 | tf_op jit(solution)/shard_map/convert_element_type | solution.py:109
  (23 shorter events, 1.0 us)
Async XLA Ops:
  6.5 52.9 %all-gather.5.cloned.1.call-start = ((), (), s32[]{:S(2)}) async-start(), calls=%async_computation | async-start | bytes 1671168 | tf_op jit(solution)/shard_map/all_gather | solution.py:64
  7.3 96.0 %all-gather.7.cloned.1.call-start = ((), (), s32[]{:S(2)}) async-start(), calls=%async_computation.1 | async-start | bytes 1114112 | tf_op jit(solution)/shard_map/all_gather | solution.py:84
  8.0 301.6 %all-reduce.3.cloned.1.call-start = ((), (), s32[]{:S(2)}) async-start(), calls=%async_computation.2 | async-start | bytes 9437184 | tf_op jit(solution)/shard_map/psum | solution.py:89
  108.1 1.4 copy-start.2
  108.1 277.6 %all-gather.9.cloned.1.call-start = ((), (), s32[]{:S(2)}) async-start(), calls=%async_computation.3 | async-start | bytes 8912896 | tf_op jit(solution)/shard_map/all_gather | solution.py:94
  108.7 333.4 %all-gather.11.cloned.1.call-start = ((), (), s32[]{:S(2)}) async-start(), calls=%async_computation.4 | async-start | bytes 4456448 | tf_op jit(solution)/shard_map/all_gather | solution.py:103
  109.3 542.5 %all-reduce.5.cloned.1.call-start = ((), (), s32[]{:S(2)}) async-start(), calls=%async_computation.5 | async-start | bytes 9437184 | tf_op jit(solution)/shard_map/psum | solution.py:107
  316.1 2.2 copy-start
  385.8 10.4 %copy-start.1 = (bf16[3,384,2048]{2,1,0:T(8,128)(2,1)S(1)}, bf16[3,384,2048]{2,1,0:T(8,128)(2,1)}, u32[]{:S(2)}) copy-start(bf16[3,384,2048]{2,1,0:T(8,128)(2,1)} %fusion.4) | copy-start | bytes 14155780
Sparse Core Ops, SparseCore 0:
  9.8 49.6 all-gather.4
  61.7 41.4 all-gather.6
  108.3 201.3 all-reduce.2
  312.0 73.7 all-gather.8
  387.9 54.2 all-gather.10
  452.7 199.0 all-reduce.4
where the time goes:
time: 668 us
  waiting for transfers between devices  578 us (87%)
  matrix products  37.9 us (6%)
  other arithmetic  23.8 us (4%)
  local copies, waits for them, and re-layouts  14.3 us (2%)
  between operations  13.6 us (2%)
    psum x1, waiting for transfers between devices, shards(): lax.psum(attn_terms.astype(jnp.bfloat16), 'tp').astype(jnp.float32)  200 us
    psum x1, waiting for transfers between devices, shards(): mlp = lax.psum(mlp_terms.astype(jnp.bfloat16), 'tp').astype(jnp.float32)  199 us
    all_gather x1, waiting for transfers between devices, shards(): block_piece = lax.all_gather(gate_up_weight, 'var', axis=0, tiled=True)  64.5 us
    all_gather x1, waiting for transfers between devices, shards(): lax.all_gather(qkv_weight, 'var', axis=0, tiled=True)  47.8 us
    all_gather x1, waiting for transfers between devices, shards(): lax.all_gather(out_weight, 'var', axis=1, tiled=True)  32.4 us
    all_gather x1, waiting for transfers between devices, shards(): lax.all_gather(down_weight, 'var', axis=1, tiled=True)  31.4 us
    dot_general x1, matrix products, shards(): jnp.dot(columns, flat_piece, preferred_element_type=jnp.float32)  14.6 us
  transfers between devices with their start and end apart: 6, of which 6 were waited for; matrix products, arithmetic and copies ran while one was open for 7% of the time, Pallas kernels for 0%

commit v1 on v0

--- a/solution.py
+++ b/solution.py
@@ -91,7 +91,9 @@
     mlp_input = rms_norm(whole_after)
     flat_mlp = mlp_input.reshape(row_count, model_width)
     ff_local = gate_up_weight.shape[2]
-    block_piece = lax.all_gather(gate_up_weight, "var", axis=0, tiled=True)
+    block_piece = jnp.concatenate(
+        lax.all_to_all(jnp.stack([gate_up_weight] * lax.axis_size("var")), "var", 0, 0), axis=0
+    )
     columns = flat_mlp
     flat_piece = block_piece.reshape(block_piece.shape[0], 2 * ff_local)
     gate_and_up = jnp.dot(columns, flat_piece, preferred_element_type=jnp.float32)

time: 668 us -> 678 us (1.015)
  local copies, waits for them, and re-layouts: 14.3 us -> 22.1 us
    psum x1, waiting for transfers between devices: 200 us -> 270 us  [shards(): lax.psum(attn_terms.astype(jnp.bfloat16), 'tp').astype(jnp.float32)]
    all_gather x1 -> x0, waiting for transfers between devices: 64.5 us -> none  [shards(): block_piece = lax.all_gather(gate_up_weight, 'var', axis=0, tiled=True)]
    all_gather x1, waiting for transfers between devices: 31.4 us -> 22.8 us  [shards(): lax.all_gather(down_weight, 'var', axis=1, tiled=True)]
    another operation x0 -> x1, local copies, waits for them, and re-layouts: none -> 7.61 us  [shards(): jnp.stack([gate_up_weight] * lax.axis_size('var'))]
  transfers between devices with their start and end apart: 6 -> 6, of which waited for: 6 -> 5; matrix products, arithmetic and copies ran while one was open for 7% -> 8% of each run, Pallas kernels for 0% -> 0%
where the time goes in v1:
time: 678 us; the launch traced here: 677 us
  waiting for transfers between devices  574 us (85%)
  matrix products  37.9 us (6%)
  other arithmetic  23.8 us (4%)
  local copies, waits for them, and re-layouts  22.1 us (3%)
  between operations  13.2 us (2%)
    psum x1, waiting for transfers between devices, shards(): lax.psum(attn_terms.astype(jnp.bfloat16), 'tp').astype(jnp.float32)  270 us
    psum x1, waiting for transfers between devices, shards(): mlp = lax.psum(mlp_terms.astype(jnp.bfloat16), 'tp').astype(jnp.float32)  199 us
    all_gather x1, waiting for transfers between devices, shards(): lax.all_gather(qkv_weight, 'var', axis=0, tiled=True)  47.8 us
    all_gather x1, waiting for transfers between devices, shards(): lax.all_gather(out_weight, 'var', axis=1, tiled=True)  32.4 us
    all_gather x1, waiting for transfers between devices, shards(): lax.all_gather(down_weight, 'var', axis=1, tiled=True)  22.8 us
    dot_general x1, matrix products, shards(): jnp.dot(columns, flat_piece, preferred_element_type=jnp.float32)  14.6 us
  transfers between devices with their start and end apart: 6, of which 5 were waited for; matrix products, arithmetic and copies ran while one was open for 8% of the time, Pallas kernels for 0%

profile of v1, /device:TPU:1, one launch (start us, length us, event | category | flops | bytes accessed | tf_op | source)
XLA Modules:
  0.0 677.2 jit_solution(10957432547419688870)
XLA Ops:
  6.5 0.7 all-gather.4.cloned.1.call-update
  7.3 0.7 all-gather.6.cloned.1.call-update
  8.1 3.3 fusion
  11.7 47.8 %all-gather.4.cloned.1.call-done = bf16[2048,384]{1,0:T(8,128)(2,1)} async-done(((bf16[128,384]{1,0:T(8,128)(2,1)}), bf16[2048,384]{1,0:T(8,128)(2,1)}) %all-gather.4.cloned.1.call-update) | async-done | bytes 1572880 | tf_op jit(solution)/shard_map/all_gather | solution.py:64
  59.5 1.7 copy.7
  61.2 4.6 fusion.9
  66.1 1.2 fusion.7
  67.3 1.5 fusion.6
  68.8 2.1 fusion.17
  70.9 32.4 %all-gather.6.cloned.1.call-done = bf16[256,2048]{1,0:T(8,128)(2,1)} async-done(((bf16[256,128]{1,0:T(8,128)(2,1)}), bf16[256,2048]{1,0:T(8,128)(2,1)}) %all-gather.6.cloned.1.call-update) | async-done | bytes 1048592 | tf_op jit(solution)/shard_map/all_gather | solution.py:84
  103.3 4.9 convolution_convert_fusion.1
  108.2 7.6 %stack.2 = bf16[16,128,2,1024]{3,2,1,0:T(2,128)(2,1)} broadcast(bf16[128,2,1024]{2,1,0:T(2,128)(2,1)S(1)} %copy-done.2), dimensions={1,2,3} | broadcast | bytes 8912896 | tf_op jit(solution)/shard_map/stack | solution.py:95
  115.8 5.9 all-to-all-start
  121.8 0.5 all-gather.8.cloned.1.call-update
  122.6 269.9 %all-reduce.3.cloned.1.call-done = bf16[3,384,2048]{2,1,0:T(8,128)(2,1)} async-done(((bf16[3,384,2048]{2,1,0:T(8,128)(2,1)}), bf16[3,384,2048]{2,1,0:T(8,128)(2,1)}) %all-reduce.3.cloned.1.call-update) | async-done | bytes 4718608 | tf_op jit(solution)/shard_map/psum | solution.py:89
  392.5 6.5 fusion.3
  399.0 2.2 copy-done
  401.1 3.0 fusion.4
  404.1 10.6 %copy.20 = bf16[256,8,2,1024]{3,1,2,0:T(8,128)(2,1)} copy(bf16[256,8,2,1024]{3,2,1,0:T(2,128)(2,1)} %bitcast.35) | data formatting | bytes 16777216
  414.7 14.6 %fusion.41 = f32[1152,2048]{1,0:T(8,128)} fusion(bf16[1152,2048]{1,0:T(8,128)(2,1)S(1)} %bitcast.100, bf16[2048,2048]{1,0:T(8,128)(2,1)} %bitcast.98), kind=kOutput, calls=%fused_computation.62 | convolution fusion | flops 9663676416 | bytes 22544384 | tf_op jit(solution)/shard_map/dot_general | solution.py:99
  429.3 22.8 %all-gather.8.cloned.1.call-done = bf16[1024,2048]{1,0:T(8,128)(2,1)} async-done(((bf16[1024,128]{1,0:T(8,128)(2,1)}), bf16[1024,2048]{1,0:T(8,128)(2,1)}) %all-gather.8.cloned.1.call-update) | async-done | bytes 4194320 | tf_op jit(solution)/shard_map/all_gather | solution.py:105
  452.1 10.4 %convolution_convert_fusion = bf16[1152,2048]{1,0:T(8,128)(2,1)} fusion(bf16[1024,2048]{1,0:T(8,128)(2,1)} %all-gather.8.cloned.1.call-done, f32[1152,2048]{1,0:T(8,128)} %fusion.41), kind=kOutput, calls=%fused_computation.12 | convolution fusion | flops 4841275392 | bytes 18350080 | tf_op jit(solution)/shard_map/dot_general | solution.py:103
  462.6 199.2 %all-reduce.5.cloned.1.call-done = bf16[3,384,2048]{2,1,0:T(8,128)(2,1)} async-done(((bf16[3,384,2048]{2,1,0:T(8,128)(2,1)}), bf16[3,384,2048]{2,1,0:T(8,128)(2,1)}) %all-reduce.5.cloned.1.call-update) | async-done | bytes 4718608 | tf_op jit(solution)/shard_map/psum | solution.py:109
  661.8 8.9 %fusion.5 = bf16[3,384,2048]{2,1,0:T(8,128)(2,1)} fusion(bf16[3,384,2048]{2,1,0:T(8,128)(2,1)} %copy-done, bf16[3,384,2048]{2,1,0:T(8,128)(2,1)} %all-reduce.5.cloned.1.call-done, f32[3]{0:T(128)S(1)} %get-tuple-element.9), kind=kLoop, calls=%fused_computation.11 | loop fusion | flops 11796480 | bytes 14155788 | tf_op jit(solution)/shard_map/convert_element_type | solution.py:111
  (25 shorter events, 1.0 us)
Async XLA Ops:
  6.5 52.9 %all-gather.4.cloned.1.call-start = ((), (), s32[]{:S(2)}) async-start(), calls=%async_computation.1 | async-start | bytes 1671168 | tf_op jit(solution)/shard_map/all_gather | solution.py:64
  7.3 96.0 %all-gather.6.cloned.1.call-start = ((), (), s32[]{:S(2)}) async-start(), calls=%async_computation.2 | async-start | bytes 1114112 | tf_op jit(solution)/shard_map/all_gather | solution.py:84
  8.0 384.5 %all-reduce.3.cloned.1.call-start = ((), (), s32[]{:S(2)}) async-start(), calls=%async_computation.3 | async-start | bytes 9437184 | tf_op jit(solution)/shard_map/psum | solution.py:89
  103.3 4.9 copy-start.2
  115.8 6.7 copy-start.3
  115.8 288.3 %all-to-all-start = ((bf16[16,128,2,1024]{3,2,1,0:T(2,128)(2,1)}), bf16[16,128,2,1024]{3,2,1,0:T(2,128)(2,1)}, u32[]{:S(2)}, u32[]{:S(2)}) async-start(bf16[16,128,2,1024]{3,2,1,0:T(2,128)(2,1)} %stack.2), calls=%async_computation | async-start | bytes 16777216 | tf_op jit(solution)/shard_map/all_to_all | solution.py:95
  121.7 330.4 %all-gather.8.cloned.1.call-start = ((), (), s32[]{:S(2)}) async-start(), calls=%async_computation.4 | async-start | bytes 4456448 | tf_op jit(solution)/shard_map/all_gather | solution.py:105
  122.3 539.5 %all-reduce.5.cloned.1.call-start = ((), (), s32[]{:S(2)}) async-start(), calls=%async_computation.5 | async-start | bytes 9437184 | tf_op jit(solution)/shard_map/psum | solution.py:109
  398.9 2.2 copy-start
  404.1 10.6 %copy-start.1 = (bf16[3,384,2048]{2,1,0:T(8,128)(2,1)S(1)}, bf16[3,384,2048]{2,1,0:T(8,128)(2,1)}, u32[]{:S(2)}) copy-start(bf16[3,384,2048]{2,1,0:T(8,128)(2,1)} %fusion.4) | copy-start | bytes 14155780
Sparse Core Ops, SparseCore 0:
  9.8 49.6 all-gather.3
  61.7 41.4 all-gather.5
  108.3 284.0 all-reduce.2
  394.6 57.5 all-gather.7
  462.7 199.0 all-reduce.4
